TPU v7x, 128 devices: a whole 4x4x4 slice. The times are simulated.
128 devices in a mesh: ctx: 16 (over z_hi, x, core), tp: 8 (over z_lo, y).
Axes of the slice: x: 4, y: 4, z: 4 (z_hi: 2, z_lo: 2; z = z_hi * 2 + z_lo), core: 2. Of those that a mesh axis runs over, the one named last changes fastest.
Arguments:
- query_gate: bfloat16 [32, 1048576], P('tp', 'ctx'), may hold values from -6 to 6
- key_branch: bfloat16 [32, 1048576], P('tp', 'ctx'), may hold values from -6 to 6
- value_branch: bfloat16 [32, 1048576], P('tp', 'ctx'), may hold values from -6 to 6
- long_filter: float32 [32, 1048576], P('tp', 'ctx'), may hold values from -0.005859375 to 0.005859375
- skip_gain: float32 [32], P('tp'), may hold values from 0.5 to 1.5
- out_weight: bfloat16 [32, 32], replicated, may hold values from -1 to 1
Outputs:
- mixed: bfloat16 [32, 1048576], P('tp', 'ctx')
All inputs are finite; a program needn't handle non-finite values.
Results may differ from a plain program's by a relative error of at most 0.02.
Values may be sent and summed in bfloat16 or wider, within the bound.
A program may use at most 256 MiB of HBM per device.

v0:
```python
import math

import jax
import jax.numpy as jnp
from jax import lax
from jax.sharding import PartitionSpec as P

FACTOR = 128


def turn_table(left_idx, right_idx, length, sign):
    phase = left_idx[:, None] * right_idx[None, :] % length
    angle = sign * 2.0 * math.pi / length * phase.astype(jnp.float32)
    return (jnp.cos(angle), jnp.sin(angle))


def apply_form(form, table, values):
    return jnp.einsum(form, table, values, precision=lax.Precision.HIGHEST)


def apply_complex(form, tab_re, tab_im, val_re, val_im, table_first):
    if table_first:
        out_re = apply_form(form, tab_re, val_re) - apply_form(form, tab_im, val_im)
        out_im = apply_form(form, tab_re, val_im) + apply_form(form, tab_im, val_re)
    else:
        out_re = apply_form(form, val_re, tab_re) - apply_form(form, val_im, tab_im)
        out_im = apply_form(form, val_im, tab_re) + apply_form(form, val_re, tab_im)
    return (out_re, out_im)


def times_table(val_re, val_im, tab_re, tab_im):
    return (val_re * tab_re - val_im * tab_im, val_re * tab_im + val_im * tab_re)


def local_forward(val_re, val_im, width_a, width_b):
    iota_a = jnp.arange(width_a, dtype=jnp.int32)
    iota_b = jnp.arange(width_b, dtype=jnp.int32)
    fb_re, fb_im = turn_table(iota_b, iota_b, width_b, -1.0)
    step_re, step_im = apply_complex("cb,...ba->...ca", fb_re, fb_im, val_re, val_im, True)
    tw_re, tw_im = turn_table(iota_b, iota_a, width_a * width_b, -1.0)
    step_re, step_im = times_table(step_re, step_im, tw_re, tw_im)
    fa_re, fa_im = turn_table(iota_a, iota_a, width_a, -1.0)
    return apply_complex("...ca,ad->...cd", fa_re, fa_im, step_re, step_im, False)


def local_inverse(val_re, val_im, width_a, width_b):
    iota_a = jnp.arange(width_a, dtype=jnp.int32)
    iota_b = jnp.arange(width_b, dtype=jnp.int32)
    fa_re, fa_im = turn_table(iota_a, iota_a, width_a, 1.0)
    step_re, step_im = apply_complex("...cd,da->...ca", fa_re, fa_im, val_re, val_im, False)
    tw_re, tw_im = turn_table(iota_b, iota_a, width_a * width_b, 1.0)
    step_re, step_im = times_table(step_re, step_im, tw_re, tw_im)
    fb_re, fb_im = turn_table(iota_b, iota_b, width_b, 1.0)
    return apply_complex("bc,...ca->...ba", fb_re, fb_im, step_re, step_im, True)


def local(query_gate, key_branch, value_branch, long_filter, skip_gain, out_weight):
    ctx_count = lax.axis_size("ctx")
    ctx_index = lax.axis_index("ctx")
    chans, tok_count = query_gate.shape
    width_a = FACTOR
    width_b = tok_count // FACTOR
    residues = 2 * ctx_count
    fft_length = residues * tok_count
    signal = key_branch.astype(jnp.float32) * value_branch.astype(jnp.float32)
    stacked = jnp.concatenate([signal, long_filter], 0)[:, None, :]
    blocks = lax.all_to_all(
        stacked.astype(jnp.bfloat16), "ctx", split_axis=2, concat_axis=1, tiled=True
    ).astype(stacked.dtype)
    dev_idx = jnp.arange(ctx_count, dtype=jnp.int32)
    second_res = jnp.where(dev_idx == 0, ctx_count, residues - dev_idx)
    res_order = jnp.stack([dev_idx, second_res], 1).reshape(residues)
    blk_idx = jnp.arange(ctx_count, dtype=jnp.int32)
    cross_re, cross_im = turn_table(res_order, blk_idx, residues, -1.0)
    spec_re = apply_form("kn,snm->skm", cross_re, blocks)
    spec_im = apply_form("kn,snm->skm", cross_im, blocks)
    spec_re, spec_im = (
        lax.all_to_all(
            spec_re.astype(jnp.bfloat16), "ctx", split_axis=1, concat_axis=2, tiled=True
        ).astype(spec_re.dtype),
        lax.all_to_all(
            spec_im.astype(jnp.bfloat16), "ctx", split_axis=1, concat_axis=2, tiled=True
        ).astype(spec_im.dtype),
    )
    own_res = jnp.stack([ctx_index, jnp.where(ctx_index == 0, ctx_count, residues - ctx_index)])
    offsets = jnp.arange(tok_count, dtype=jnp.int32)
    tw_re, tw_im = turn_table(own_res, offsets, fft_length, -1.0)
    spec_re, spec_im = times_table(spec_re, spec_im, tw_re, tw_im)
    series = spec_re.shape[0]
    spec_re = spec_re.reshape(series, 2, width_b, width_a)
    spec_im = spec_im.reshape(series, 2, width_b, width_a)
    spec_re, spec_im = local_forward(spec_re, spec_im, width_a, width_b)
    sig_re, sig_im = (spec_re[:chans], spec_im[:chans])
    fil_re, fil_im = (spec_re[chans:], spec_im[chans:])
    prod_re, prod_im = times_table(sig_re, sig_im, fil_re, fil_im)
    back_re, back_im = local_inverse(prod_re, prod_im, width_a, width_b)
    back_re = back_re.reshape(chans, 2, tok_count)
    back_im = back_im.reshape(chans, 2, tok_count)
    inv_re, inv_im = turn_table(own_res, offsets, fft_length, 1.0)
    back_re, back_im = times_table(back_re, back_im, inv_re, inv_im)
    back_re = back_re * (1.0 / fft_length)
    back_im = back_im * (1.0 / fft_length)
    block_rows = jnp.arange(1 * lax.axis_size("ctx"), dtype=jnp.int32)
    row_re, row_im = turn_table(block_rows, own_res, residues, 1.0)
    conv = lax.psum_scatter(
        (
            apply_form("nj,cjm->ncm", row_re, back_re) - apply_form("nj,cjm->ncm", row_im, back_im)
        ).astype(jnp.bfloat16),
        "ctx",
        scatter_dimension=0,
        tiled=True,
    ).astype(jnp.float32)[0]
    gated = (query_gate.astype(jnp.float32) * (conv + skip_gain[:, None] * signal)).astype(
        jnp.bfloat16
    )
    tp_index = lax.axis_index("tp")
    out_dev = out_weight.shape[1] // lax.axis_size("tp")
    own_cols = lax.dynamic_slice_in_dim(out_weight, tp_index * out_dev, out_dev, 1)
    mixed = jnp.dot(
        own_cols.T,
        lax.all_gather(gated, "tp", axis=0, tiled=True),
        preferred_element_type=jnp.float32,
    )
    return mixed.astype(jnp.bfloat16)


def solution(mesh):
    placed = (P("tp", "ctx"), P("tp", "ctx"), P("tp", "ctx"), P("tp", "ctx"), P("tp"), P())
    return jax.shard_map(
        local, mesh=mesh, in_specs=placed, out_specs=P("tp", "ctx"), check_vma=False
    )
```

profile of v0, /device:TPU:0, one launch (start us, length us, event | category | flops | bytes accessed | tf_op | source)
XLA Modules:
  0.0 1102.1 jit_solution(4058956443266954925)
XLA Ops:
  6.5 2.0 fusion.52
  8.5 0.5 pad_maximum_fusion
  9.1 49.8 %copy.64 = bf16[8,1,65536]{0,1,2:T(2,128)(2,1)} copy(bf16[8,1,65536]{2,0,1:T(8,128)(2,1)S(1)} %pad_maximum_fusion) | data formatting | bytes 2097152 | tf_op jit(solution)/shard_map/concatenate | solution.py:66
  58.9 0.5 broadcast.406
  59.4 355.8 %reduce = bf16[65536,8]{1,0:T(8,128)(2,1)} reduce(bf16[65536,1,8]{2,1,0:T(2,128)(2,1)} %bitcast.149, bf16[]{:T(256)} %broadcast.406), dimensions={1}, to_apply=%bitcast.134.reduce_sub_computation | reduce | bytes 2097154
  415.2 20.6 %reshape.239 = bf16[16,2,16384]{2,1,0:T(2,128)(2,1)} reshape(bf16[65536,8]{1,0:T(8,128)(2,1)} %reduce) | data formatting | bytes 2097152
  435.8 8.0 all-to-all-start
  443.8 0.1 copy.66
  443.9 0.1 mul.566
  444.0 17.8 %all-to-all-done = bf16[16,2,16384]{2,1,0:T(2,128)(2,1)S(1)} async-done(((bf16[16,2,16384]{2,1,0:T(2,128)(2,1)}), bf16[16,2,16384]{2,1,0:T(2,128)(2,1)S(1)}, u32[]{:S(2)}, u32[]{:S(2)}) %all-to-all-start) | async-done | bytes 1048608 | tf_op jit(solution)/shard_map/all_to_all | solution.py:67
  461.8 39.4 %reshape.240 = bf16[65536,1,8]{2,1,0:T(2,128)(2,1)} reshape(bf16[16,2,16384]{2,1,0:T(2,128)(2,1)S(1)} %all-to-all-done) | data formatting | bytes 2097152
  501.2 58.6 %copy.65 = bf16[8,1,65536]{2,0,1:T(8,128)(2,1)S(1)} copy(bf16[8,1,65536]{0,1,2:T(2,128)(2,1)} %bitcast.150) | data formatting | bytes 2097152 | tf_op jit(solution)/shard_map/all_to_all | solution.py:67
  559.8 2.0 fusion.2
  561.8 2.5 copy.69
  564.3 3.7 all-to-all-start.2
  568.0 0.1 pad_add_fusion.1
  568.1 2.0 fusion.1
  570.1 2.6 copy.67
  572.7 24.5 %all-to-all-done.2 = bf16[8,32,4096]{2,0,1:T(8,128)(2,1)S(1)} async-done(((bf16[8,32,4096]{2,0,1:T(8,128)(2,1)}), bf16[8,32,4096]{2,0,1:T(8,128)(2,1)S(1)}, u32[]{:S(2)}, u32[]{:S(2)}) %all-to-all-start.2) | async-done | bytes 2097184 | tf_op jit(solution)/shard_map/all_to_all | solution.py:81
  597.2 4.9 all-to-all-start.1
  602.1 0.3 all-reduce.3.cloned.1.call-start
  602.4 8.9 fusion.77
  611.3 1.0 multiply_sine_fusion.6
  612.2 0.9 copy.80
  613.1 1.0 multiply_cosine_fusion.6
  614.1 0.8 copy.79
  614.9 1.7 multiply_sine_fusion.7
  616.7 2.1 fusion.81
  618.8 4.8 copy.119
  623.6 4.9 reshape.220
  628.5 2.9 all-to-all-done.1
  631.4 4.8 copy.120
  636.2 5.3 reshape.219
  641.5 21.0 %fusion.34 = f32[8,2,128,512]{3,2,1,0:T(8,128)S(1)} fusion(f32[8,2,512,128]{3,2,1,0:T(8,128)} %reshape.220, f32[8,2,512,128]{3,2,1,0:T(8,128)} %reshape.219, f32[2,512,128]{2,1,0:T(8,128)S(1)} %get-tuple-element.8, f32[2,512,128]{2,1,0:T(8,128)S(1)} %get-tuple-element.7), kind=kOutput, calls=%fused_computation.61 | convolution fusion | flops 6449266688 | bytes 13631488 | tf_op jit(solution)/shard_map/cb,...ba->...ca/dot_general | solution.py:18
  662.6 17.3 %fusion.36 = f32[8,2,128,512]{3,2,1,0:T(8,128)S(1)} fusion(f32[8,2,512,128]{3,2,1,0:T(8,128)S(1)} %copy-done.1, f32[8,2,512,128]{3,2,1,0:T(8,128)S(1)} %copy-done.2, f32[2,512,128]{2,1,0:T(8,128)S(1)} %get-tuple-element.8, f32[2,512,128]{2,1,0:T(8,128)S(1)} %get-tuple-element.7), kind=kOutput, calls=%fused_computation.63 | convolution fusion | flops 6449266688 | bytes 13631488 | tf_op jit(solution)/shard_map/cb,...ba->...ca/dot_general | solution.py:18
  679.8 17.7 %convolution_add_fusion.1 = f32[8,2,128,512]{3,2,1,0:T(8,128)S(1)} fusion(f32[8,2,128,512]{3,2,1,0:T(8,128)S(1)} %fusion.34, f32[8,2,512,128]{3,2,1,0:T(8,128)S(1)} %copy-done.1, f32[8,2,512,128]{3,2,1,0:T(8,128)S(1)} %copy-done.2, f32[2,512,128]{2,1,0:T(8,128)S(1)} %get-tuple-element.8, f32[2,512,128]{2,1,0:T(8,128)S(1)} %get-tuple-element.7), kind=kOutput, calls=%fused_computation.19 | convolution fusion | flops 6450315264 | bytes 17825792 | tf_op jit(solution)/shard_map/cb,...ba->...ca/dot_general | solution.py:18
  697.5 17.3 %convolution_subtract_fusion.2 = f32[8,2,128,512]{3,2,1,0:T(8,128)S(1)} fusion(f32[8,2,128,512]{3,2,1,0:T(8,128)S(1)} %fusion.36, f32[8,2,512,128]{3,2,1,0:T(8,128)S(1)} %copy-done.1, f32[8,2,512,128]{3,2,1,0:T(8,128)S(1)} %copy-done.2, f32[2,512,128]{2,1,0:T(8,128)S(1)} %get-tuple-element.8, f32[2,512,128]{2,1,0:T(8,128)S(1)} %get-tuple-element.7), kind=kOutput, calls=%fused_computation.20 | convolution fusion | flops 6450315264 | bytes 17825792 | tf_op jit(solution)/shard_map/cb,...ba->...ca/dot_general | solution.py:18
  714.9 7.6 fusion.14
  722.5 7.4 fusion.18
  729.9 7.2 convolution_add_fusion
  737.1 7.4 convolution_subtract_fusion.1
  744.6 0.5 multiply_subtract_fusion.2
  745.1 2.1 fusion.87
  747.2 2.1 fusion.89
  749.4 2.1 convolution_add_fusion.2
  751.5 2.5 convolution_subtract_fusion.3
  754.1 10.6 fusion.28
  764.6 11.8 %fusion.30 = f32[4,2,128,512]{3,2,1,0:T(8,128)} fusion(f32[4,2,512,128]{3,2,1,0:T(8,128)S(1)} %convolution_add_fusion.2, f32[4,2,512,128]{3,2,1,0:T(8,128)S(1)} %convolution_subtract_fusion.3, f32[512,128]{1,0:T(8,128)S(1)} %copy-done.8, f32[512,128]{1,0:T(8,128)S(1)} %copy-done.9), kind=kOutput, calls=%fused_computation.57 | convolution fusion | flops 3226468352 | bytes 6815744 | tf_op jit(solution)/shard_map/bc,...ca->...ba/dot_general | solution.py:18
  776.4 12.0 %add_bitcast_fusion = f32[4,2,512,128]{2,3,1,0:T(8,128)} fusion(f32[4,2,128,512]{3,2,1,0:T(8,128)S(1)} %fusion.28, f32[4,2,512,128]{3,2,1,0:T(8,128)S(1)} %convolution_add_fusion.2, f32[4,2,512,128]{3,2,1,0:T(8,128)S(1)} %convolution_subtract_fusion.3, f32[512,128]{1,0:T(8,128)S(1)} %copy-done.8, f32[512,128]{1,0:T(8,128)S(1)} %copy-done.9), kind=kOutput, calls=%fused_computation.29 | convolution fusion | flops 3226992640 | bytes 8912896 | tf_op jit(solution)/shard_map/bc,...ca->...ba/dot_general | solution.py:18
  788.4 3.0 copy.86
  791.4 4.4 reshape.218
  795.8 14.4 %subtract_bitcast_fusion = f32[4,2,512,128]{2,3,1,0:T(8,128)} fusion(f32[4,2,128,512]{3,2,1,0:T(8,128)} %fusion.30, f32[4,2,512,128]{3,2,1,0:T(8,128)S(1)} %convolution_add_fusion.2, f32[4,2,512,128]{3,2,1,0:T(8,128)} %copy-done.3, f32[512,128]{1,0:T(8,128)S(1)} %copy-done.8, f32[512,128]{1,0:T(8,128)} %copy.79), kind=kOutput, calls=%fused_computation.31 | convolution fusion | flops 3226992640 | bytes 8912896 | tf_op jit(solution)/shard_map/bc,...ca->...ba/dot_general | solution.py:18
  810.2 3.0 copy.83
  813.2 4.4 reshape.217
  817.6 17.5 %fusion.9 = f32[16,4,65536]{2,0,1:T(8,128)S(1)} fusion(f32[4,2,65536]{2,1,0:T(2,128)S(1)} %copy-done.4, f32[4,2,65536]{2,1,0:T(2,128)} %reshape.217, f32[2,65536]{1,0:T(2,128)S(1)} %get-tuple-element.10, f32[2,65536]{1,0:T(2,128)S(1)} %get-tuple-element.9, s32[2]{0:T(128)S(1)} %pad_add_fusion.1), kind=kOutput, calls=%fused_computation.25 | convolution fusion | flops 102760896 | bytes 22020104 | tf_op jit(solution)/shard_map/nj,cjm->ncm/dot_general | solution.py:18
  835.1 18.1 %fusion = bf16[16,4,65536]{2,0,1:T(8,128)(2,1)S(1)} fusion(f32[16,4,65536]{2,0,1:T(8,128)S(1)} %fusion.9, f32[4,2,65536]{2,1,0:T(2,128)S(1)} %copy-done.4, f32[4,2,65536]{2,1,0:T(2,128)S(1)} %copy-done.5, f32[2,65536]{1,0:T(2,128)S(1)} %get-tuple-element.10, f32[2,65536]{1,0:T(2,128)S(1)} %get-tuple-element.9, s32[2]{0:T(128)S(1)} %pad_add_fusion.1), kind=kOutput, calls=%fused_computation.1 | convolution fusion | flops 111149504 | bytes 30408712 | tf_op jit(solution)/shard_map/nj,cjm->ncm/dot_general | solution.py:18
  853.2 13.0 %copy.87 = bf16[16,4,65536]{2,1,0:T(4,128)(2,1)} copy(bf16[16,4,65536]{2,0,1:T(8,128)(2,1)S(1)} %fusion) | data formatting | bytes 16777216 | tf_op jit(solution)/shard_map/convert_element_type | solution.py:108
  866.3 0.6 copy-done.14
  866.8 0.7 dynamic-slice
  867.5 162.2 %all-reduce.3.cloned.1.call-done = bf16[16,4,65536]{2,1,0:T(4,128)(2,1)} async-done(((bf16[16,4,65536]{2,1,0:T(4,128)(2,1)}), bf16[16,4,65536]{2,1,0:T(4,128)(2,1)}) %all-reduce.3.cloned.1.call-update) | async-done | bytes 8388624
  1029.7 3.3 fusion.56
  1033.1 53.0 %all-gather.3.cloned.1.call-done = bf16[8,4,65536]{2,1,0:T(4,128)(2,1)} async-done(((bf16[1,4,65536]{2,1,0:T(4,128)(2,1)}), bf16[8,4,65536]{2,1,0:T(4,128)(2,1)}) %all-gather.3.cloned.1.call-update) | async-done | bytes 4194320 | tf_op jit(solution)/shard_map/all_gather | solution.py:121
  1086.1 5.2 reshape.225
  1091.3 3.8 convolution_convert_fusion
  (36 shorter events, 0.2 us)
Async XLA Ops:
  6.5 1084.8 %copy-start = (bf16[32,32]{1,0:T(8,128)(2,1)S(1)}, bf16[32,32]{1,0:T(8,128)(2,1)}, u32[]{:S(2)}) copy-start(bf16[32,32]{1,0:T(8,128)(2,1)} %param.11) | copy-start | bytes 6148
  435.8 26.0 %all-to-all-start = ((bf16[16,2,16384]{2,1,0:T(2,128)(2,1)}), bf16[16,2,16384]{2,1,0:T(2,128)(2,1)S(1)}, u32[]{:S(2)}, u32[]{:S(2)}) async-start(bf16[16,2,16384]{2,1,0:T(2,128)(2,1)} %reshape.239), calls=%async_computation | async-start | bytes 2097152 | tf_op jit(solution)/shard_map/all_to_all | solution.py:67
  564.3 32.9 %all-to-all-start.2 = ((bf16[8,32,4096]{2,0,1:T(8,128)(2,1)}), bf16[8,32,4096]{2,0,1:T(8,128)(2,1)S(1)}, u32[]{:S(2)}, u32[]{:S(2)}) async-start(bf16[8,32,4096]{2,0,1:T(8,128)(2,1)} %copy.69), calls=%async_computation.2 | async-start | bytes 4194304 | tf_op jit(solution)/shard_map/all_to_all | solution.py:81
  597.2 17.7 %copy-start.6 = (bf16[8,32,4096]{2,0,1:T(8,128)(2,1)}, bf16[8,32,4096]{2,0,1:T(8,128)(2,1)S(1)}, u32[]{:S(2)}) copy-start(bf16[8,32,4096]{2,0,1:T(8,128)(2,1)S(1)} %all-to-all-done.2) | copy-start | bytes 6291460
  597.2 34.2 %all-to-all-start.1 = ((bf16[8,32,4096]{2,0,1:T(8,128)(2,1)}), bf16[8,32,4096]{2,0,1:T(8,128)(2,1)}, u32[]{:S(2)}, u32[]{:S(2)}) async-start(bf16[8,32,4096]{2,0,1:T(8,128)(2,1)} %copy.67), calls=%async_computation.1 | async-start | bytes 4194304 | tf_op jit(solution)/shard_map/all_to_all | solution.py:78
  602.1 427.6 %all-reduce.3.cloned.1.call-start = ((), (), s32[]{:S(2)}) async-start(), calls=%async_computation.4 | async-start | bytes 16777216
  641.5 21.0 %copy-start.1 = (f32[8,2,512,128]{3,2,1,0:T(8,128)S(1)}, f32[8,2,512,128]{3,2,1,0:T(8,128)}, u32[]{:S(2)}) copy-start(f32[8,2,512,128]{3,2,1,0:T(8,128)} %reshape.220) | copy-start | bytes 12582916
  641.5 21.0 %copy-start.2 = (f32[8,2,512,128]{3,2,1,0:T(8,128)S(1)}, f32[8,2,512,128]{3,2,1,0:T(8,128)}, u32[]{:S(2)}) copy-start(f32[8,2,512,128]{3,2,1,0:T(8,128)} %reshape.219) | copy-start | bytes 12582916
  697.5 17.4 %copy-start.7 = (f32[512,128]{0,1:T(8,128)S(1)}, f32[512,128]{0,1:T(8,128)}, u32[]{:S(2)}) copy-start(f32[512,128]{0,1:T(8,128)} %get-tuple-element.14) | copy-start | bytes 786436
  751.5 2.5 copy-start.8
  751.5 2.5 copy-start.9
  754.0 22.4 %copy-start.3 = (f32[4,2,512,128]{3,2,1,0:T(8,128)}, f32[4,2,512,128]{3,2,1,0:T(8,128)S(1)}, u32[]{:S(2)}) copy-start(f32[4,2,512,128]{3,2,1,0:T(8,128)S(1)} %convolution_subtract_fusion.3) | copy-start | bytes 6291460
  810.2 7.4 copy-start.4
  817.6 17.5 %copy-start.5 = (f32[4,2,65536]{2,1,0:T(2,128)S(1)}, f32[4,2,65536]{2,1,0:T(2,128)}, u32[]{:S(2)}) copy-start(f32[4,2,65536]{2,1,0:T(2,128)} %reshape.217) | copy-start | bytes 6291460
  866.2 0.7 copy-start.14
  866.2 163.5 %copy-start.10 = (bf16[4,65536]{1,0:T(4,128)(2,1)S(1)}, bf16[4,65536]{1,0:T(4,128)(2,1)}, u32[]{:S(2)}) copy-start(bf16[4,65536]{1,0:T(4,128)(2,1)} %param.8) | copy-start | bytes 1572868
  866.2 163.5 %copy-start.11 = (bf16[4,65536]{1,0:T(4,128)(2,1)S(1)}, bf16[4,65536]{1,0:T(4,128)(2,1)}, u32[]{:S(2)}) copy-start(bf16[4,65536]{1,0:T(4,128)(2,1)} %param.7) | copy-start | bytes 1572868
  866.2 163.5 %copy-start.12 = (bf16[4,65536]{1,0:T(4,128)(2,1)S(1)}, bf16[4,65536]{1,0:T(4,128)(2,1)}, u32[]{:S(2)}) copy-start(bf16[4,65536]{1,0:T(4,128)(2,1)} %param.6) | copy-start | bytes 1572868
  866.2 163.5 %copy-start.13 = (f32[4]{0:T(128)S(1)}, f32[4]{0:T(128)}, u32[]{:S(2)}) copy-start(f32[4]{0:T(128)} %param.10) | copy-start | bytes 52
  866.2 219.9 %all-gather.3.cloned.1.call-start = ((), (), s32[]{:S(2)}) async-start(), calls=%async_computation.3 | async-start | bytes 4718592 | tf_op jit(solution)/shard_map/all_gather | solution.py:121
Sparse Core Ops, SparseCore 0:
  866.3 163.3 all-reduce.2
  1033.2 52.8 all-gather.2
where the time goes:
time: 1110 us; the launch traced here: 1100 us
  other arithmetic  377 us (34%)
  waiting for transfers between devices  260 us (23%)
  local copies, waits for them, and re-layouts  230 us (21%)
  matrix products  204 us (18%)
  starting transfers between devices  16.9 us (2%)
  between operations  14 us (1%)
    unnamed x2, other arithmetic  359 us
    dot_general x20, matrix products, apply_form(): return jnp.einsum(form, table, values, precision=lax.Precision.HIGHEST)  200 us
    unnamed x3, waiting for transfers between devices  162 us
    unnamed x35, local copies, waits for them, and re-layouts  67 us
    all_to_all x1, local copies, waits for them, and re-layouts, local(): lax.all_to_all(stacked.astype(jnp.bfloat16), 'ctx', split_axis=2, concat_...  58.6 us
    all_gather x1, waiting for transfers between devices, local(): lax.all_gather(gated, 'tp', axis=0, tiled=True)  53 us
    concatenate x1, local copies, waits for them, and re-layouts, local(): stacked = jnp.concatenate([signal, long_filter], 0)[:, None, :]  49.8 us
    all_to_all x1, waiting for transfers between devices, local(): lax.all_to_all(spec_im.astype(jnp.bfloat16), 'ctx', split_axis=1, concat_...  24.5 us
  transfers between devices with their start and end apart: 5, of which 5 were waited for; matrix products, arithmetic and copies ran while one was open for 3% of the time, Pallas kernels for 0%

commit v1 on v0

v1 whole, which is shorter than its diff:
```python
import functools
import math

import jax
import jax.numpy as jnp
import ml_dtypes
import numpy as np
from jax import lax
from jax.experimental import pallas as pl
from jax.experimental.pallas import tpu as pltpu
from jax.sharding import PartitionSpec as P

CTX = 16
TP = 8
CH = 4
FA = 512
FB = 128
M = FA * FB
ROWS = FA // CTX
SLAB = FA // TP
BF = jnp.bfloat16
F32 = jnp.float32


def phase(numer, denom):
    ang = -2.0 * math.pi * (numer % denom) / denom
    return np.cos(ang), np.sin(ang)


@functools.cache
def tables():
    f1 = 4 * np.arange(FA, dtype=np.int64) + 1
    a_re, a_im = phase(f1[:, None] * np.arange(FA)[None, :], 4 * FA)
    fwd_a = np.concatenate([a_re, a_im], 0).astype(ml_dtypes.bfloat16)
    inv_a = np.ascontiguousarray(fwd_a.T)
    t_re, t_im = phase(f1[:, None] * np.arange(FB)[None, :], 4 * M)
    turn = np.stack([t_re, t_im]).astype(np.float32)
    b_re, b_im = phase(np.arange(FB)[:, None] * np.arange(FB)[None, :], FB)
    fwd_b = np.block([[b_re, b_im], [-b_im, b_re]]).astype(ml_dtypes.bfloat16)
    inv_b = np.ascontiguousarray(fwd_b.T)
    return fwd_a, inv_a, turn, fwd_b, inv_b


def dot(left, right):
    return jnp.dot(left, right, preferred_element_type=F32)


def forward_kernel(k_ref, v_ref, h_ref, fa_ref, tw_ref, fb_ref, out_ref, sig):
    sig[...] = k_ref[...].astype(F32) * v_ref[...].astype(F32)
    for c in range(CH):
        s = sig[pl.ds(c, FA, stride=CH), :].astype(BF)
        h = h_ref[pl.ds(c, FA, stride=CH), :].astype(BF)
        step = dot(fa_ref[...], jnp.concatenate([s, h], 1))
        for i, row in ((0, c), (1, CH + c)):
            a_re = step[:FA, i * FB : (i + 1) * FB]
            a_im = step[FA:, i * FB : (i + 1) * FB]
            z_re = a_re * tw_ref[0] - a_im * tw_ref[1]
            z_im = a_re * tw_ref[1] + a_im * tw_ref[0]
            z = jnp.concatenate([z_re.astype(BF), z_im.astype(BF)], 1)
            spec = dot(z, fb_ref[...]).astype(BF)
            out_ref[:, row] = spec.reshape(CTX, ROWS, 2 * FB)


def block_kernel(in_ref, out_ref):
    tile = 8
    for c in range(CH):

        @pl.loop(0, ROWS // 16)
        def _(i):
            r = pl.ds(pl.multiple_of(i * 16, 16), 16)
            for half in range(2):
                sl = slice(half * tile, half * tile + tile)
                g_re, g_im = [], []
                p_re = p_im = None
                for n in range(CTX):
                    blk = in_ref[n, CH + c, r, :][sl].astype(F32)
                    h_re, h_im = blk[:, :FB], blk[:, FB:]
                    if n == 0:
                        g_re.append(h_re)
                        g_im.append(h_im)
                    else:
                        g_re.append(h_re - p_im)
                        g_im.append(h_im + p_re)
                    p_re, p_im = h_re, h_im
                y_re = [None] * CTX
                y_im = [None] * CTX
                for n in range(CTX):
                    blk = in_ref[n, c, r, :][sl].astype(F32)
                    s_re, s_im = blk[:, :FB], blk[:, FB:]
                    for j in range(CTX - n):
                        t_re = s_re * g_re[j] - s_im * g_im[j]
                        t_im = s_re * g_im[j] + s_im * g_re[j]
                        o = n + j
                        y_re[o] = t_re if y_re[o] is None else y_re[o] + t_re
                        y_im[o] = t_im if y_im[o] is None else y_im[o] + t_im
                for n in range(CTX):
                    out_ref[n, c, pl.ds(pl.multiple_of(i * 16 + half * tile, tile), tile), :] = (
                        jnp.concatenate([y_re[n], y_im[n]], 1).astype(BF)
                    )


def inverse_kernel(skip_ref, y_ref, q_ref, k_ref, v_ref, ia_ref, tw_ref, ib_ref, out_ref, sig, gate):
    sig[...] = k_ref[...].astype(F32) * v_ref[...].astype(F32)
    gate[...] = q_ref[...].astype(F32)
    for pair in range(CH // 2):
        cols = []
        for c in (2 * pair, 2 * pair + 1):
            y = y_ref[:, c].reshape(FA, 2 * FB)
            w = dot(y, ib_ref[...]) * (1.0 / M)
            w_re, w_im = w[:, :FB], w[:, FB:]
            v_re = w_re * tw_ref[0] + w_im * tw_ref[1]
            v_im = w_im * tw_ref[0] - w_re * tw_ref[1]
            cols.append(jnp.concatenate([v_re.astype(BF), v_im.astype(BF)], 0))
        conv = dot(ia_ref[...], jnp.concatenate(cols, 1))
        for i, c in ((0, 2 * pair), (1, 2 * pair + 1)):
            s = sig[pl.ds(c, FA, stride=CH), :]
            q = gate[pl.ds(c, FA, stride=CH), :]
            gated = q * (conv[:, i * FB : (i + 1) * FB] + skip_ref[c] * s)
            out_ref[:, c] = gated.astype(BF).reshape(TP, SLAB, FB)


def iota(shape, dim):
    return lax.broadcasted_iota(jnp.int32, shape, dim)


def mix_kernel(w_ref, g_ref, out_ref):
    chans = TP * CH
    size = chans * 16
    row, col = iota((size, chans), 0), iota((size, chans), 1)
    pick_out = (row // 64 * CH + row % CH == col).astype(F32).astype(BF)
    spread = (iota((chans, size), 1) // 16 == iota((chans, size), 0)).astype(F32).astype(BF)
    w_t = w_ref[...].astype(F32).T.astype(BF)
    wide = dot(dot(pick_out, w_t).astype(BF), spread)
    same = iota((size, size), 0) // CH % 16 == iota((size, size), 1) % 16
    table = jnp.where(same, wide, 0.0).astype(BF)
    for g in range(SLAB // 16):
        x = g_ref[:, g * 16 : (g + 1) * 16, :].reshape(size, FB)
        out_ref[:, g * 64 : (g + 1) * 64, :] = dot(table, x).astype(BF).reshape(TP, 64, FB)


def rows_of(x):
    return x.reshape(CH, FA, FB).transpose(1, 0, 2).reshape(FA * CH, FB)


def vmem(n):
    return [pl.BlockSpec(memory_space=pltpu.VMEM)] * n


def params():
    return pltpu.CompilerParams(vmem_limit_bytes=48 * 1024 * 1024)


def local(query_gate, key_branch, value_branch, long_filter, skip_gain, out_weight):
    fwd_a, inv_a, turn, fwd_b, inv_b = (jnp.asarray(t) for t in tables())
    q, k, v, h = (rows_of(x) for x in (query_gate, key_branch, value_branch, long_filter))
    spec = pl.pallas_call(
        forward_kernel,
        out_shape=jax.ShapeDtypeStruct((CTX, 2 * CH, ROWS, 2 * FB), BF),
        in_specs=vmem(6),
        out_specs=pl.BlockSpec(memory_space=pltpu.VMEM),
        scratch_shapes=[pltpu.VMEM((CH * FA, FB), F32)],
        compiler_params=params(),
        name="forward",
    )(k, v, h, fwd_a, turn, fwd_b)
    spec = lax.all_to_all(spec, "ctx", split_axis=0, concat_axis=0, tiled=True)
    prod = pl.pallas_call(
        block_kernel,
        out_shape=jax.ShapeDtypeStruct((CTX, CH, ROWS, 2 * FB), BF),
        in_specs=vmem(1),
        out_specs=pl.BlockSpec(memory_space=pltpu.VMEM),
        compiler_params=params(),
        name="blocks",
    )(spec)
    prod = lax.all_to_all(prod, "ctx", split_axis=0, concat_axis=0, tiled=True)
    gated = pl.pallas_call(
        inverse_kernel,
        out_shape=jax.ShapeDtypeStruct((TP, CH, SLAB, FB), BF),
        in_specs=[pl.BlockSpec(memory_space=pltpu.SMEM)] + vmem(7),
        out_specs=pl.BlockSpec(memory_space=pltpu.VMEM),
        scratch_shapes=[pltpu.VMEM((CH * FA, FB), F32)] * 2,
        compiler_params=params(),
        name="inverse",
    )(skip_gain, prod, q, k, v, inv_a, turn, inv_b)
    gated = lax.all_to_all(gated, "tp", split_axis=0, concat_axis=0, tiled=True)
    mixed = pl.pallas_call(
        mix_kernel,
        out_shape=jax.ShapeDtypeStruct((TP, SLAB * CH, FB), BF),
        in_specs=vmem(2),
        out_specs=pl.BlockSpec(memory_space=pltpu.VMEM),
        compiler_params=params(),
        name="mix",
    )(out_weight, gated.reshape(TP * CH, SLAB, FB))
    mixed = lax.all_to_all(mixed, "tp", split_axis=0, concat_axis=0, tiled=True)
    return mixed.reshape(FA, CH, FB).transpose(1, 0, 2).reshape(CH, M)


def solution(mesh):
    placed = (P("tp", "ctx"), P("tp", "ctx"), P("tp", "ctx"), P("tp", "ctx"), P("tp"), P())
    return jax.shard_map(
        local, mesh=mesh, in_specs=placed, out_specs=P("tp", "ctx"), check_vma=False
    )
```

time: 1110 us -> 99.9 us (0.09)
  other arithmetic: 377 us -> 0 us
  waiting for transfers between devices: 260 us -> 0 us
  local copies, waits for them, and re-layouts: 230 us -> 7.31 us
  matrix products: 204 us -> 0 us
  blocking collectives: 0 us -> 83.1 us
  starting transfers between devices: 16.9 us -> 0 us
  between operations: 14 us -> 0.11 us
    unnamed x2 -> x0, other arithmetic: 359 us -> none
    dot_general x21 -> x0, matrix products: 204 us -> none  [the longest x20 200 us: apply_form(): return jnp.einsum(form, table, values, precision=lax.Precision.HIGHEST)]
    unnamed x3 -> x0, waiting for transfers between devices: 162 us -> none
    all_to_all x0 -> x4, blocking collectives: none -> 83.1 us  [the longest x1 36.8 us: local(): spec = lax.all_to_all(spec, 'ctx', split_axis=0, concat_axis=0, tiled=True)]
    unnamed x35 -> x29, local copies, waits for them, and re-layouts: 67 us -> 7.31 us
    all_to_all x1 -> x0, local copies, waits for them, and re-layouts: 58.6 us -> none  [local(): lax.all_to_all(stacked.astype(jnp.bfloat16), 'ctx', split_axis=2, concat_...]
    all_gather x1 -> x0, waiting for transfers between devices: 53 us -> none  [local(): lax.all_gather(gated, 'tp', axis=0, tiled=True)]
    concatenate x1 -> x0, local copies, waits for them, and re-layouts: 49.8 us -> none  [local(): stacked = jnp.concatenate([signal, long_filter], 0)[:, None, :]]
  transfers between devices with their start and end apart: 5 -> 0, of which waited for: 5 -> 0; matrix products, arithmetic and copies ran while one was open for 3% -> 0% of each run, Pallas kernels for 0% -> 0%
where the time goes in v1:
time: 99.9 us; the launch traced here: 99.4 us
  blocking collectives  83.1 us (83%)
  Pallas kernels  8.84 us (9%)
  local copies, waits for them, and re-layouts  7.31 us (7%)
    all_to_all x1, blocking collectives, local(): spec = lax.all_to_all(spec, 'ctx', split_axis=0, concat_axis=0, tiled=True)  36.8 us
    all_to_all x1, blocking collectives, local(): prod = lax.all_to_all(prod, 'ctx', split_axis=0, concat_axis=0, tiled=True)  20.6 us
    all_to_all x1, blocking collectives, local(): gated = lax.all_to_all(gated, 'tp', split_axis=0, concat_axis=0, tiled=True)  14.4 us
    all_to_all x1, blocking collectives, local(): mixed = lax.all_to_all(mixed, 'tp', split_axis=0, concat_axis=0, tiled=True)  11.3 us
    unnamed x29, local copies, waits for them, and re-layouts  7.31 us
    pallas_call x1, Pallas kernels, local(): pl.pallas_call(forward_kernel, out_shape=jax.ShapeDtypeStruct((CTX, 2 * C...  3.41 us
    pallas_call x1, Pallas kernels, local(): pl.pallas_call(block_kernel, out_shape=jax.ShapeDtypeStruct((CTX, CH, ROW...  2.54 us

profile of v1, /device:TPU:0, one launch (start us, length us, event | category | flops | bytes accessed | tf_op | source)
XLA Modules:
  0.0 99.4 jit_solution(7058293123263670488)
XLA Ops:
  0.0 0.0 copy-start
  0.0 1.0 %copy-done = bf16[4,65536]{1,0:T(4,128)(2,1)S(1)} copy-done((bf16[4,65536]{1,0:T(4,128)(2,1)S(1)}, bf16[4,65536]{1,0:T(4,128)(2,1)}, u32[]{:S(2)}) %copy-start) | copy-done | bytes 524312
  1.0 0.0 copy-start.2
  1.0 1.0 %copy-done.2 = bf16[4,65536]{1,0:T(4,128)(2,1)S(1)} copy-done((bf16[4,65536]{1,0:T(4,128)(2,1)S(1)}, bf16[4,65536]{1,0:T(4,128)(2,1)}, u32[]{:S(2)}) %copy-start.2) | copy-done | bytes 524312
  2.1 0.0 copy-start.4
  2.1 1.0 %copy-done.4 = f32[2,512,128]{2,1,0:T(8,128)S(1)} copy-done((f32[2,512,128]{2,1,0:T(8,128)S(1)}, f32[2,512,128]{2,1,0:T(8,128)}, u32[]{:S(2)}) %copy-start.4) | copy-done | bytes 524312
  3.1 0.0 copy-start.7
  3.1 1.2 %copy-done.7 = f32[4,65536]{1,0:T(4,128)S(1)} copy-done((f32[4,65536]{1,0:T(4,128)S(1)}, f32[4,65536]{1,0:T(4,128)}, u32[]{:S(2)}) %copy-start.7) | copy-done | bytes 1048600
  4.4 0.0 copy-start.8
  4.4 1.2 %copy-done.8 = bf16[1024,512]{1,0:T(8,128)(2,1)S(1)} copy-done((bf16[1024,512]{1,0:T(8,128)(2,1)S(1)}, bf16[1024,512]{1,0:T(8,128)(2,1)}, u32[]{:S(2)}) %copy-start.8) | copy-done | bytes 1048600
  5.6 0.0 copy-start.11
  5.6 0.9 copy-done.11
  6.5 3.4 %forward.1 = bf16[16,8,32,256]{3,2,1,0:T(8,128)(2,1)S(1)} custom-call(bf16[2048,128]{1,0:T(8,128)(2,1)S(1)} %bitcast.26, bf16[2048,128]{1,0:T(8,128)(2,1)S(1)} %bitcast.28, f32[2048,128]{1,0:T(8,128)S(1)} %bitcast.31, bf16[1024,512]{1,0:T(8,128)(2,1)S(1)} %copy-done.8, f32[2,512,128]{2,1,0:T(8,128)S(1)} %copy-done.4, bf16[256,256]{1,0:T(8,128)(2,1)S(1)} %copy-done.11), custom_call_target="tpu_custom_call" | custom-call | tf_op jit(solution)/shard_map/forward/pallas_call | solution.py:156
  9.9 36.8 %all_to_all.20.in_ref = bf16[16,8,32,256]{3,2,1,0:T(8,128)(2,1)S(1)} all-to-all(bf16[16,8,32,256]{3,2,1,0:T(8,128)(2,1)S(1)} %forward.1), channel_id=1, replica_groups=mesh['ctx'=16,'tp'=8] {'ctx'}, dimensions={0} | all-to-all | bytes 4194304 | tf_op jit(solution)/shard_map/all_to_all | solution.py:165
  46.7 0.0 copy-start.1
  46.7 0.0 copy-start.3
  46.7 0.0 copy-start.5
  46.7 0.0 copy-start.6
  46.7 0.0 copy-start.9
  46.7 0.0 copy-start.10
  46.8 0.0 copy-start.13
  46.8 2.5 %blocks.1 = bf16[16,4,32,256]{3,2,1,0:T(8,128)(2,1)S(1)} custom-call(bf16[16,8,32,256]{3,2,1,0:T(8,128)(2,1)S(1)} %all_to_all.20.in_ref), custom_call_target="tpu_custom_call" | custom-call | tf_op jit(solution)/shard_map/blocks/pallas_call | solution.py:166
  49.3 20.6 %all_to_all.21.y_ref = bf16[16,4,32,256]{3,2,1,0:T(8,128)(2,1)S(1)} all-to-all(bf16[16,4,32,256]{3,2,1,0:T(8,128)(2,1)S(1)} %blocks.1), channel_id=1, replica_groups=mesh['ctx'=16,'tp'=8] {'ctx'}, dimensions={0} | all-to-all | bytes 2097152 | tf_op jit(solution)/shard_map/all_to_all | solution.py:174
  69.9 0.0 copy-done.1
  69.9 0.0 copy-done.3
  69.9 0.0 copy-done.5
  69.9 0.0 copy-done.6
  69.9 0.0 copy-done.9
  69.9 0.0 copy-done.10
  70.0 0.0 copy-done.13
  70.0 0.0 copy-start.12
  70.0 1.9 %inverse.1 = bf16[8,4,64,128]{3,2,1,0:T(8,128)(2,1)S(1)} custom-call(f32[4]{0:T(128)S(1)} %copy-done.13, bf16[16,4,32,256]{3,2,1,0:T(8,128)(2,1)S(1)} %all_to_all.21.y_ref, bf16[2048,128]{1,0:T(8,128)(2,1)S(1)} %bitcast.32, bf16[2048,128]{1,0:T(8,128)(2,1)S(1)} %bitcast.27, bf16[2048,128]{1,0:T(8,128)(2,1)S(1)} %bitcast.29, bf16[512,1024]{1,0:T(8,128)(2,1)S(1)} %copy-done.6, ...), custom_call_target="tpu_custom_call" | custom-call | tf_op jit(solution)/shard_map/inverse/pallas_call | solution.py:175
  71.9 14.4 %all_to_all.22 = bf16[8,4,64,128]{3,2,1,0:T(8,128)(2,1)S(1)} all-to-all(bf16[8,4,64,128]{3,2,1,0:T(8,128)(2,1)S(1)} %inverse.1), channel_id=1, replica_groups=mesh['ctx'=16,'tp'=8] {'tp'}, dimensions={0} | all-to-all | bytes 1048576 | tf_op jit(solution)/shard_map/all_to_all | solution.py:184
  86.3 0.0 copy-done.12
  86.3 1.0 %mix.1 = bf16[8,256,128]{2,1,0:T(8,128)(2,1)S(1)} custom-call(bf16[32,32]{1,0:T(8,128)(2,1)S(1)} %copy-done.12, bf16[32,64,128]{2,1,0:T(8,128)(2,1)S(1)} %bitcast.30), custom_call_target="tpu_custom_call" | custom-call | tf_op jit(solution)/shard_map/mix/pallas_call | solution.py:185
  87.3 11.3 %all_to_all.23 = bf16[8,256,128]{2,1,0:T(8,128)(2,1)S(1)} all-to-all(bf16[8,256,128]{2,1,0:T(8,128)(2,1)S(1)} %mix.1), channel_id=1, replica_groups=mesh['ctx'=16,'tp'=8] {'tp'}, dimensions={0} | all-to-all | bytes 1048576 | tf_op jit(solution)/shard_map/all_to_all | solution.py:193
  98.6 0.8 copy.18
Async XLA Ops:
  0.0 1.0 %copy-start = (bf16[4,65536]{1,0:T(4,128)(2,1)S(1)}, bf16[4,65536]{1,0:T(4,128)(2,1)}, u32[]{:S(2)}) copy-start(bf16[4,65536]{1,0:T(4,128)(2,1)} %param.12) | copy-start | bytes 1572868
  1.0 1.0 %copy-start.2 = (bf16[4,65536]{1,0:T(4,128)(2,1)S(1)}, bf16[4,65536]{1,0:T(4,128)(2,1)}, u32[]{:S(2)}) copy-start(bf16[4,65536]{1,0:T(4,128)(2,1)} %param.13) | copy-start | bytes 1572868
  2.1 1.0 %copy-start.4 = (f32[2,512,128]{2,1,0:T(8,128)S(1)}, f32[2,512,128]{2,1,0:T(8,128)}, u32[]{:S(2)}) copy-start(f32[2,512,128]{2,1,0:T(8,128)} %constant.12.clone.tw_ref) | copy-start | bytes 1572868
  3.1 1.2 %copy-start.7 = (f32[4,65536]{1,0:T(4,128)S(1)}, f32[4,65536]{1,0:T(4,128)}, u32[]{:S(2)}) copy-start(f32[4,65536]{1,0:T(4,128)} %param.14) | copy-start | bytes 3145732
  4.4 1.2 %copy-start.8 = (bf16[1024,512]{1,0:T(8,128)(2,1)S(1)}, bf16[1024,512]{1,0:T(8,128)(2,1)}, u32[]{:S(2)}) copy-start(bf16[1024,512]{1,0:T(8,128)(2,1)} %constant.10.clone.fa_ref) | copy-start | bytes 3145732
  5.6 0.9 copy-start.11
  46.7 23.2 %copy-start.1 = (bf16[4,65536]{1,0:T(4,128)(2,1)S(1)}, bf16[4,65536]{1,0:T(4,128)(2,1)}, u32[]{:S(2)}) copy-start(bf16[4,65536]{1,0:T(4,128)(2,1)} %param.12) | copy-start | bytes 1572868
  46.7 23.2 %copy-start.3 = (bf16[4,65536]{1,0:T(4,128)(2,1)S(1)}, bf16[4,65536]{1,0:T(4,128)(2,1)}, u32[]{:S(2)}) copy-start(bf16[4,65536]{1,0:T(4,128)(2,1)} %param.13) | copy-start | bytes 1572868
  46.7 23.2 %copy-start.5 = (f32[2,512,128]{2,1,0:T(8,128)S(1)}, f32[2,512,128]{2,1,0:T(8,128)}, u32[]{:S(2)}) copy-start(f32[2,512,128]{2,1,0:T(8,128)} %constant.12.clone.tw_ref) | copy-start | bytes 1572868
  46.7 23.2 %copy-start.6 = (bf16[512,1024]{1,0:T(8,128)(2,1)S(1)}, bf16[512,1024]{1,0:T(8,128)(2,1)}, u32[]{:S(2)}) copy-start(bf16[512,1024]{1,0:T(8,128)(2,1)} %constant.11.clone.ia_ref) | copy-start | bytes 3145732
  46.7 23.2 %copy-start.9 = (bf16[4,65536]{1,0:T(4,128)(2,1)S(1)}, bf16[4,65536]{1,0:T(4,128)(2,1)}, u32[]{:S(2)}) copy-start(bf16[4,65536]{1,0:T(4,128)(2,1)} %param.11) | copy-start | bytes 1572868
  46.7 23.2 %copy-start.10 = (bf16[256,256]{1,0:T(8,128)(2,1)S(1)}, bf16[256,256]{1,0:T(8,128)(2,1)}, u32[]{:S(2)}) copy-start(bf16[256,256]{1,0:T(8,128)(2,1)} %constant.14.clone.ib_ref) | copy-start | bytes 393220
  46.8 23.2 %copy-start.13 = (f32[4]{0:T(128)S(1)}, f32[4]{0:T(128)}, u32[]{:S(2)}) copy-start(f32[4]{0:T(128)} %skip_ref.1) | copy-start | bytes 52
  70.0 16.3 %copy-start.12 = (bf16[32,32]{1,0:T(8,128)(2,1)S(1)}, bf16[32,32]{1,0:T(8,128)(2,1)}, u32[]{:S(2)}) copy-start(bf16[32,32]{1,0:T(8,128)(2,1)} %w_ref.1) | copy-start | bytes 6148
